TPU v7x, 32 devices: a whole 2x2x4 slice. The times are simulated.
32 devices in a mesh: grp: 2 (over y), tile: 4 (over z), sub: 4 (over x, core).
Axes of the slice: x: 2, y: 2, z: 4, core: 2. Of those that a mesh axis runs over, the one named last changes fastest.
Arguments:
- features: bfloat16 [24, 32, 1024], P(('grp', 'tile'), 'sub'), parts along dimension 0, may hold values from -6 to 6
- out_grad: bfloat16 [24, 32, 1024], P(('grp', 'tile'), 'sub'), parts along dimension 0, may hold values from -6 to 6
- filters: bfloat16 [5, 32, 32], replicated, may hold values from -0.5 to 0.5
- tile_map: int32 [12], replicated, may hold values from 0 to 11, as said below
Outputs:
- in_grad: bfloat16 [24, 32, 1024], P(('grp', 'tile'), 'sub'), parts along dimension 0
- weight_grad: float32 [10, 32, 32], P('grp', 'sub'), parts along dimension 0
There are 2 independent parts, one for each index of `grp`. A program takes and returns all parts, laid end to end along the dimension named above; an argument that names none is the same for every part. Nothing has to cross between parts.
Inputs may be any that keep to these rules, and one draw needn't show every extreme that they name: tile_map[s] is the nested index of the tile held in slot s; slots 3 * j to 3 * j + 2 lie on index j of tile and hold the nested indices 3 * j to 3 * j + 2 in some order.
All inputs are finite; a program needn't handle non-finite values.
Results may differ from a plain program's by a relative error of at most 0.00045.
Values may be sent and summed in bfloat16 or wider, within the bound.
A program may use at most 64 MiB of HBM per device.

v0:
```python
import math

import jax
import jax.numpy as jnp
import numpy as np
from jax import lax
from jax.sharding import PartitionSpec as P

K = 5


def from_behind(value, axis, steps):
    count = lax.axis_size(axis)
    pairs = [(source, (source + steps) % count) for source in range(count)]
    return lax.ppermute(value, axis, pairs)


def tile_coords(nested_code, bit_count):
    coord_x = nested_code * 0
    coord_y = nested_code * 0
    for bit_level in range(bit_count):
        coord_x = coord_x + nested_code // 4**bit_level % 2 * 2**bit_level
        coord_y = coord_y + nested_code // (2 * 4**bit_level) % 2 * 2**bit_level
    return (coord_x, coord_y)


def nested_index(coord_x, coord_y, bit_count):
    nested_code = coord_x * 0
    for bit_level in range(bit_count):
        nested_code = nested_code + coord_x // 2**bit_level % 2 * 4**bit_level
        nested_code = nested_code + coord_y // 2**bit_level % 2 * (2 * 4**bit_level)
    return nested_code


def pick(condition, when_true, when_false):
    return when_false + (when_true - when_false) * condition


def neighbour_codes(tile_ids, per_face, side_count):
    bit_count = side_count.bit_length() - 1
    face_id = tile_ids // per_face
    coord_x, coord_y = tile_coords(tile_ids % per_face, bit_count)
    column = face_id % 4
    is_north = face_id < 4
    is_south = face_id >= 8
    last_tile = side_count - 1

    def by_cycle(north_value, equator_value, south_value):
        return pick(is_north, north_value, pick(is_south, south_value, equator_value))

    side_rules = [
        (
            coord_x > 0,
            (face_id, coord_x - 1, coord_y, 1),
            (
                by_cycle(4 + column, 8 + (column + 3) % 4, 8 + (column + 3) % 4),
                by_cycle(last_tile, last_tile, coord_y),
                by_cycle(coord_y, coord_y, 0),
                by_cycle(1, 1, 2),
            ),
        ),
        (
            coord_x < last_tile,
            (face_id, coord_x + 1, coord_y, 0),
            (
                by_cycle((column + 1) % 4, column, 4 + (column + 1) % 4),
                by_cycle(coord_y, 0, 0),
                by_cycle(last_tile, coord_y, coord_y),
                by_cycle(3, 0, 0),
            ),
        ),
        (
            coord_y > 0,
            (face_id, coord_x, coord_y - 1, 3),
            (
                by_cycle(4 + (column + 1) % 4, 8 + column, 8 + (column + 1) % 4),
                by_cycle(coord_x, coord_x, 0),
                by_cycle(last_tile, last_tile, coord_x),
                by_cycle(3, 3, 0),
            ),
        ),
        (
            coord_y < last_tile,
            (face_id, coord_x, coord_y + 1, 2),
            (
                by_cycle((column + 3) % 4, (column + 3) % 4, 4 + column),
                by_cycle(last_tile, coord_x, coord_x),
                by_cycle(coord_x, 0, 0),
                by_cycle(1, 2, 2),
            ),
        ),
    ]
    target_list = []
    edge_list = []
    for inside, within, across in side_rules:
        chosen = [
            pick(inside, near_value, far_value) for near_value, far_value in zip(within, across)
        ]
        target_list.append(chosen[0] * per_face + nested_index(chosen[1], chosen[2], bit_count))
        edge_list.append(chosen[3] + tile_ids * 0)
    return (target_list, edge_list)


def neighbour_table(tile_map, per_face, side_count):
    target_list, edge_list = neighbour_codes(tile_map, per_face, side_count)
    targets = jnp.stack(target_list, axis=1).astype(jnp.int32)
    edges = jnp.stack(edge_list, axis=1).astype(jnp.int32)
    slot_of = jnp.argsort(tile_map).astype(jnp.int32)
    return (slot_of[targets].astype(jnp.int32), edges)


def peer_offsets(slot_count, device_count, per_face, side_count):
    tile_ids = np.arange(slot_count * device_count, dtype=np.int64)
    target_list, edge_list = neighbour_codes(tile_ids, per_face, side_count)
    targets = np.stack(target_list, axis=1)
    offsets = (tile_ids[:, None] // slot_count - targets // slot_count) % device_count
    distinct = sorted(set((int(value) for value in offsets.ravel())) - {0})
    position = np.zeros(device_count, dtype=np.int32)
    for order, value in enumerate(distinct):
        position[value] = order + 1
    return (distinct, position)


def edge_lines(values, tile_side):
    return jnp.stack(
        [
            values[..., :tile_side],
            values[..., -tile_side:],
            values[..., ::tile_side],
            values[..., tile_side - 1 :: tile_side],
        ],
        axis=1,
    )


def stencil(values, ghosts, tile_side):
    position = jnp.arange(values.shape[-1]) % tile_side
    zero_line = jnp.zeros_like(values[..., :1])
    upper_side = jnp.concatenate([ghosts[:, 0], values[..., :-tile_side]], axis=-1)
    lower_side = jnp.concatenate([values[..., tile_side:], ghosts[:, 1]], axis=-1)
    left_side = jnp.where(
        position == 0,
        jnp.repeat(ghosts[:, 2], tile_side, axis=-1),
        jnp.concatenate([zero_line, values[..., :-1]], axis=-1),
    )
    right_side = jnp.where(
        position == tile_side - 1,
        jnp.repeat(ghosts[:, 3], tile_side, axis=-1),
        jnp.concatenate([values[..., 1:], zero_line], axis=-1),
    )
    return -0.25 * (upper_side + lower_side + left_side + right_side)


def tile_total(filter_part):
    return lax.psum(filter_part, "tile")


def on_device(features, out_grad, filters, tile_map):
    slot_count = features.shape[0]
    group_channels = features.shape[1]
    tile_side = math.isqrt(features.shape[2])
    device_count = lax.axis_size("tile")
    total_tiles = slot_count * device_count
    side_count = math.isqrt(total_tiles // 12)
    scale_factor = 1.0 / math.sqrt(total_tiles * features.shape[2])
    highest = lax.Precision.HIGHEST
    slot_table, edge_table = neighbour_table(tile_map, total_tiles // 12, side_count)
    my_device = lax.axis_index("tile")
    first_slot = my_device * slot_count
    my_slots = lax.dynamic_slice_in_dim(slot_table, first_slot, slot_count, 0)
    my_edges = lax.dynamic_slice_in_dim(edge_table, first_slot, slot_count, 0)
    channel_start = lax.axis_index("sub") * group_channels
    weights = filters.astype(jnp.float32)
    distinct, position = peer_offsets(slot_count, device_count, total_tiles // 12, side_count)
    sender_gap = (my_device - my_slots // slot_count) % device_count
    local_rows = jnp.asarray(position)[sender_gap] * slot_count + my_slots % slot_count

    def laplace(values):
        border = edge_lines(values, tile_side).reshape(slot_count, 4, group_channels * tile_side)
        received = [border]
        for offset_value in distinct:
            received.append(from_behind(border, "tile", offset_value))
        stacked = jnp.concatenate(received, axis=0)
        stacked = stacked.reshape(stacked.shape[0], 4, group_channels, tile_side)
        ghosts = stacked[local_rows, my_edges]
        return stencil(values, ghosts, tile_side)

    whole_grad = lax.all_gather(out_grad, "sub", axis=1, tiled=True)
    cotangent = whole_grad.astype(jnp.float32)
    inputs = features.astype(jnp.float32)
    previous, current = (inputs, laplace(inputs))
    filter_terms = [
        jnp.einsum("sip,sop->io", inputs, cotangent, precision=highest),
        jnp.einsum("sip,sop->io", current, cotangent, precision=highest),
    ]
    for degree in range(2, K):
        previous, current = (current, 2.0 * laplace(current) - previous)
        filter_terms.append(jnp.einsum("sip,sop->io", current, cotangent, precision=highest))
    weight_grad = tile_total(jnp.stack(filter_terms)) * scale_factor
    row_block = lax.dynamic_slice_in_dim(weights, channel_start, group_channels, 1)

    def mixed(degree):
        return jnp.einsum("sop,io->sip", cotangent, row_block[degree], precision=highest)

    next_sum = mixed(K - 1)
    after_next = jnp.zeros_like(next_sum)
    for degree in range(K - 2, 0, -1):
        next_sum, after_next = (mixed(degree) + 2.0 * laplace(next_sum) - after_next, next_sum)
    in_grad = (mixed(0) + laplace(next_sum) - after_next).astype(jnp.bfloat16)
    return (in_grad, weight_grad)


def solution(mesh):
    placed = (P(("grp", "tile"), "sub", None), P(("grp", "tile"), "sub", None), P(), P())
    return jax.shard_map(
        on_device,
        mesh=mesh,
        in_specs=placed,
        out_specs=(P(("grp", "tile"), "sub", None), P("grp", "sub", None)),
        check_vma=False,
    )
```

profile of v0, /device:TPU:0, one launch (start us, length us, event | category | flops | bytes accessed | tf_op | source)
XLA Modules:
  0.0 89.9 jit_solution(3915343842741492382)
XLA Ops:
  0.7 0.8 fusion.100
  2.1 3.1 %collective-permute-start.12 = (f32[3,4,256]{2,0,1:T(4,128)S(1)}, f32[3,4,256]{2,0,1:T(4,128)S(1)}, u32[]{:S(2)}, u32[]{:S(2)}) collective-permute-start(f32[3,4,256]{2,0,1:T(4,128)S(1)} %constant_dynamic-update-slice_fusion.16), channel_id=1, source_target_pairs={{0,4},{4,8},{8,12},{12,0},{1,5},{5,9},{9,13},{13,1},{2,6},{6,10},{... | collective-permute-start | bytes 36872 | tf_op jit(solution)/shard_map/ppermute | solution.py:15
  5.2 2.6 %collective-permute-start.13 = (f32[3,4,256]{2,0,1:T(4,128)S(1)}, f32[3,4,256]{2,0,1:T(4,128)S(1)}, u32[]{:S(2)}, u32[]{:S(2)}) collective-permute-start(f32[3,4,256]{2,0,1:T(4,128)S(1)} %constant_dynamic-update-slice_fusion.16), channel_id=1, source_target_pairs={{0,8},{4,12},{8,0},{12,4},{1,9},{5,13},{9,1},{13,5},{2,10},{6,14},... | collective-permute-start | bytes 36872 | tf_op jit(solution)/shard_map/ppermute | solution.py:15
  7.8 1.3 %collective-permute-start.14 = (f32[3,4,256]{2,0,1:T(4,128)S(1)}, f32[3,4,256]{2,0,1:T(4,128)S(1)}, u32[]{:S(2)}, u32[]{:S(2)}) collective-permute-start(f32[3,4,256]{2,0,1:T(4,128)S(1)} %constant_dynamic-update-slice_fusion.16), channel_id=1, source_target_pairs={{0,12},{4,0},{8,4},{12,8},{1,13},{5,1},{9,5},{13,9},{2,14},{6,2},{... | collective-permute-start | bytes 36872 | tf_op jit(solution)/shard_map/ppermute | solution.py:15
  9.2 5.6 %all_gather.3 = bf16[3,32,1024]{2,1,0:T(8,128)(2,1)S(1)} all-gather(bf16[3,8,1024]{2,1,0:T(8,128)(2,1)S(1)} %copy-done.2), channel_id=1, replica_groups=mesh['grp'=2,'tile'=4,'sub'=4] {'sub'}, dimensions={1}, use_global_device_ids=true | all-gather | bytes 245760 | tf_op jit(solution)/shard_map/all_gather | solution.py:188
  15.7 0.7 collective-permute-start
  18.3 1.2 %sort.17 = (s32[12]{0:T(128)}, s32[12]{0:T(128)S(1)}) sort(s32[12]{0:T(128)S(1)} %copy-done.3, s32[12]{0:T(128)S(1)} %iota.45), dimensions={0}, to_apply=%region_0.1 | sort | flops 48 | bytes 192 | tf_op jit(solution)/shard_map/jit(argsort)/sort | solution.py:108
  19.6 0.8 gather_fusion
  21.4 2.8 %collective-permute-start.2 = (f32[3,4,256]{2,0,1:T(4,128)S(1)}, f32[3,4,256]{2,0,1:T(4,128)S(1)}, u32[]{:S(2)}, u32[]{:S(2)}) collective-permute-start(f32[3,4,256]{2,0,1:T(4,128)S(1)} %constant_dynamic-update-slice_fusion), channel_id=1, source_target_pairs={{0,12},{4,0},{8,4},{12,8},{1,13},{5,1},{9,5},{13,9},{2,14},{6,2},{... | collective-permute-start | bytes 36872 | tf_op jit(solution)/shard_map/ppermute | solution.py:15
  27.3 1.5 %collective-permute-start.16 = (f32[3,4,256]{2,0,1:T(4,128)S(1)}, f32[3,4,256]{2,0,1:T(4,128)S(1)}, u32[]{:S(2)}, u32[]{:S(2)}) collective-permute-start(f32[3,4,256]{2,0,1:T(4,128)S(1)} %constant_dynamic-update-slice_fusion.20), channel_id=1, source_target_pairs={{0,8},{4,12},{8,0},{12,4},{1,9},{5,13},{9,1},{13,5},{2,10},{6,14},... | collective-permute-start | bytes 36872 | tf_op jit(solution)/shard_map/ppermute | solution.py:15
  29.0 2.9 %collective-permute-start.17 = (f32[3,4,256]{2,0,1:T(4,128)S(1)}, f32[3,4,256]{2,0,1:T(4,128)S(1)}, u32[]{:S(2)}, u32[]{:S(2)}) collective-permute-start(f32[3,4,256]{2,0,1:T(4,128)S(1)} %constant_dynamic-update-slice_fusion.20), channel_id=1, source_target_pairs={{0,12},{4,0},{8,4},{12,8},{1,13},{5,1},{9,5},{13,9},{2,14},{6,2},{... | collective-permute-start | bytes 36872 | tf_op jit(solution)/shard_map/ppermute | solution.py:15
  34.4 1.0 %collective-permute-start.4 = (f32[3,4,256]{2,0,1:T(4,128)S(1)}, f32[3,4,256]{2,0,1:T(4,128)S(1)}, u32[]{:S(2)}, u32[]{:S(2)}) collective-permute-start(f32[3,4,256]{2,0,1:T(4,128)S(1)} %constant_dynamic-update-slice_fusion.4), channel_id=1, source_target_pairs={{0,8},{4,12},{8,0},{12,4},{1,9},{5,13},{9,1},{13,5},{2,10},{6,14},... | collective-permute-start | bytes 36872 | tf_op jit(solution)/shard_map/ppermute | solution.py:15
  35.8 2.9 %collective-permute-start.5 = (f32[3,4,256]{2,0,1:T(4,128)S(1)}, f32[3,4,256]{2,0,1:T(4,128)S(1)}, u32[]{:S(2)}, u32[]{:S(2)}) collective-permute-start(f32[3,4,256]{2,0,1:T(4,128)S(1)} %constant_dynamic-update-slice_fusion.4), channel_id=1, source_target_pairs={{0,12},{4,0},{8,4},{12,8},{1,13},{5,1},{9,5},{13,9},{2,14},{6,2},{... | collective-permute-start | bytes 36872 | tf_op jit(solution)/shard_map/ppermute | solution.py:15
  41.8 1.5 %collective-permute-start.19 = (f32[3,4,256]{2,0,1:T(4,128)S(1)}, f32[3,4,256]{2,0,1:T(4,128)S(1)}, u32[]{:S(2)}, u32[]{:S(2)}) collective-permute-start(f32[3,4,256]{2,0,1:T(4,128)S(1)} %constant_dynamic-update-slice_fusion.24), channel_id=1, source_target_pairs={{0,8},{4,12},{8,0},{12,4},{1,9},{5,13},{9,1},{13,5},{2,10},{6,14},... | collective-permute-start | bytes 36872 | tf_op jit(solution)/shard_map/ppermute | solution.py:15
  43.5 2.9 %collective-permute-start.20 = (f32[3,4,256]{2,0,1:T(4,128)S(1)}, f32[3,4,256]{2,0,1:T(4,128)S(1)}, u32[]{:S(2)}, u32[]{:S(2)}) collective-permute-start(f32[3,4,256]{2,0,1:T(4,128)S(1)} %constant_dynamic-update-slice_fusion.24), channel_id=1, source_target_pairs={{0,12},{4,0},{8,4},{12,8},{1,13},{5,1},{9,5},{13,9},{2,14},{6,2},{... | collective-permute-start | bytes 36872 | tf_op jit(solution)/shard_map/ppermute | solution.py:15
  48.9 1.0 %collective-permute-start.7 = (f32[3,4,256]{2,0,1:T(4,128)S(1)}, f32[3,4,256]{2,0,1:T(4,128)S(1)}, u32[]{:S(2)}, u32[]{:S(2)}) collective-permute-start(f32[3,4,256]{2,0,1:T(4,128)S(1)} %constant_dynamic-update-slice_fusion.8), channel_id=1, source_target_pairs={{0,8},{4,12},{8,0},{12,4},{1,9},{5,13},{9,1},{13,5},{2,10},{6,14},... | collective-permute-start | bytes 36872 | tf_op jit(solution)/shard_map/ppermute | solution.py:15
  50.3 2.9 %collective-permute-start.8 = (f32[3,4,256]{2,0,1:T(4,128)S(1)}, f32[3,4,256]{2,0,1:T(4,128)S(1)}, u32[]{:S(2)}, u32[]{:S(2)}) collective-permute-start(f32[3,4,256]{2,0,1:T(4,128)S(1)} %constant_dynamic-update-slice_fusion.8), channel_id=1, source_target_pairs={{0,12},{4,0},{8,4},{12,8},{1,13},{5,1},{9,5},{13,9},{2,14},{6,2},{... | collective-permute-start | bytes 36872 | tf_op jit(solution)/shard_map/ppermute | solution.py:15
  56.3 1.5 %collective-permute-start.22 = (f32[3,4,256]{2,0,1:T(4,128)S(1)}, f32[3,4,256]{2,0,1:T(4,128)S(1)}, u32[]{:S(2)}, u32[]{:S(2)}) collective-permute-start(f32[3,4,256]{2,0,1:T(4,128)S(1)} %constant_dynamic-update-slice_fusion.28), channel_id=1, source_target_pairs={{0,8},{4,12},{8,0},{12,4},{1,9},{5,13},{9,1},{13,5},{2,10},{6,14},... | collective-permute-start | bytes 36872 | tf_op jit(solution)/shard_map/ppermute | solution.py:15
  58.0 2.9 %collective-permute-start.23 = (f32[3,4,256]{2,0,1:T(4,128)S(1)}, f32[3,4,256]{2,0,1:T(4,128)S(1)}, u32[]{:S(2)}, u32[]{:S(2)}) collective-permute-start(f32[3,4,256]{2,0,1:T(4,128)S(1)} %constant_dynamic-update-slice_fusion.28), channel_id=1, source_target_pairs={{0,12},{4,0},{8,4},{12,8},{1,13},{5,1},{9,5},{13,9},{2,14},{6,2},{... | collective-permute-start | bytes 36872 | tf_op jit(solution)/shard_map/ppermute | solution.py:15
  63.3 1.0 %collective-permute-start.10 = (f32[3,4,256]{2,0,1:T(4,128)S(1)}, f32[3,4,256]{2,0,1:T(4,128)S(1)}, u32[]{:S(2)}, u32[]{:S(2)}) collective-permute-start(f32[3,4,256]{2,0,1:T(4,128)S(1)} %constant_dynamic-update-slice_fusion.12), channel_id=1, source_target_pairs={{0,8},{4,12},{8,0},{12,4},{1,9},{5,13},{9,1},{13,5},{2,10},{6,14},... | collective-permute-start | bytes 36872 | tf_op jit(solution)/shard_map/ppermute | solution.py:15
  64.3 0.9 %collective-permute-start.11 = (f32[3,4,256]{2,0,1:T(4,128)S(1)}, f32[3,4,256]{2,0,1:T(4,128)S(1)}, u32[]{:S(2)}, u32[]{:S(2)}) collective-permute-start(f32[3,4,256]{2,0,1:T(4,128)S(1)} %constant_dynamic-update-slice_fusion.12), channel_id=1, source_target_pairs={{0,12},{4,0},{8,4},{12,8},{1,13},{5,1},{9,5},{13,9},{2,14},{6,2},{... | collective-permute-start | bytes 36872 | tf_op jit(solution)/shard_map/ppermute | solution.py:15
  65.7 1.1 %collective-permute-start.9 = (f32[3,4,256]{2,0,1:T(4,128)S(1)}, f32[3,4,256]{2,0,1:T(4,128)S(1)}, u32[]{:S(2)}, u32[]{:S(2)}) collective-permute-start(f32[3,4,256]{2,0,1:T(4,128)S(1)} %constant_dynamic-update-slice_fusion.12), channel_id=1, source_target_pairs={{0,4},{4,8},{8,12},{12,0},{1,5},{5,9},{9,13},{13,1},{2,6},{6,10},{... | collective-permute-start | bytes 36872 | tf_op jit(solution)/shard_map/ppermute | solution.py:15
  68.7 18.3 %psum.7 = f32[5,8,32]{2,1,0:T(8,128)S(1)} all-reduce(f32[5,8,32]{2,1,0:T(8,128)S(1)} %fusion.8), channel_id=1, replica_groups=mesh['grp'=2,'tile'=4,'sub'=4] {'tile'}, use_global_device_ids=true, to_apply=%region_1.2 | all-reduce | flops 1280 | bytes 10240 | tf_op jit(solution)/shard_map/psum | solution.py:155
  89.2 0.8 fusion.7
  (247 shorter events, 26.3 us)
Async XLA Ops:
  2.1 19.3 %collective-permute-start.12 = (f32[3,4,256]{2,0,1:T(4,128)S(1)}, f32[3,4,256]{2,0,1:T(4,128)S(1)}, u32[]{:S(2)}, u32[]{:S(2)}) collective-permute-start(f32[3,4,256]{2,0,1:T(4,128)S(1)} %constant_dynamic-update-slice_fusion.16), channel_id=1, source_target_pairs={{0,4},{4,8},{8,12},{12,0},{1,5},{5,9},{9,13},{13,1},{2,6},{6,10},{... | collective-permute-start | bytes 36872 | tf_op jit(solution)/shard_map/ppermute | solution.py:15
  5.2 19.0 %collective-permute-start.13 = (f32[3,4,256]{2,0,1:T(4,128)S(1)}, f32[3,4,256]{2,0,1:T(4,128)S(1)}, u32[]{:S(2)}, u32[]{:S(2)}) collective-permute-start(f32[3,4,256]{2,0,1:T(4,128)S(1)} %constant_dynamic-update-slice_fusion.16), channel_id=1, source_target_pairs={{0,8},{4,12},{8,0},{12,4},{1,9},{5,13},{9,1},{13,5},{2,10},{6,14},... | collective-permute-start | bytes 36872 | tf_op jit(solution)/shard_map/ppermute | solution.py:15
  7.8 16.4 %collective-permute-start.14 = (f32[3,4,256]{2,0,1:T(4,128)S(1)}, f32[3,4,256]{2,0,1:T(4,128)S(1)}, u32[]{:S(2)}, u32[]{:S(2)}) collective-permute-start(f32[3,4,256]{2,0,1:T(4,128)S(1)} %constant_dynamic-update-slice_fusion.16), channel_id=1, source_target_pairs={{0,12},{4,0},{8,4},{12,8},{1,13},{5,1},{9,5},{13,9},{2,14},{6,2},{... | collective-permute-start | bytes 36872 | tf_op jit(solution)/shard_map/ppermute | solution.py:15
  15.7 13.3 %collective-permute-start = (f32[3,4,256]{2,0,1:T(4,128)S(1)}, f32[3,4,256]{2,0,1:T(4,128)S(1)}, u32[]{:S(2)}, u32[]{:S(2)}) collective-permute-start(f32[3,4,256]{2,0,1:T(4,128)S(1)} %constant_dynamic-update-slice_fusion), channel_id=1, source_target_pairs={{0,4},{4,8},{8,12},{12,0},{1,5},{5,9},{9,13},{13,1},{2,6},{6,10},{... | collective-permute-start | bytes 36872 | tf_op jit(solution)/shard_map/ppermute | solution.py:15
  16.4 15.5 %collective-permute-start.1 = (f32[3,4,256]{2,0,1:T(4,128)S(1)}, f32[3,4,256]{2,0,1:T(4,128)S(1)}, u32[]{:S(2)}, u32[]{:S(2)}) collective-permute-start(f32[3,4,256]{2,0,1:T(4,128)S(1)} %constant_dynamic-update-slice_fusion), channel_id=1, source_target_pairs={{0,8},{4,12},{8,0},{12,4},{1,9},{5,13},{9,1},{13,5},{2,10},{6,14},... | collective-permute-start | bytes 36872 | tf_op jit(solution)/shard_map/ppermute | solution.py:15
  21.4 10.5 %collective-permute-start.2 = (f32[3,4,256]{2,0,1:T(4,128)S(1)}, f32[3,4,256]{2,0,1:T(4,128)S(1)}, u32[]{:S(2)}, u32[]{:S(2)}) collective-permute-start(f32[3,4,256]{2,0,1:T(4,128)S(1)} %constant_dynamic-update-slice_fusion), channel_id=1, source_target_pairs={{0,12},{4,0},{8,4},{12,8},{1,13},{5,1},{9,5},{13,9},{2,14},{6,2},{... | collective-permute-start | bytes 36872 | tf_op jit(solution)/shard_map/ppermute | solution.py:15
  26.7 9.2 %collective-permute-start.15 = (f32[3,4,256]{2,0,1:T(4,128)S(1)}, f32[3,4,256]{2,0,1:T(4,128)S(1)}, u32[]{:S(2)}, u32[]{:S(2)}) collective-permute-start(f32[3,4,256]{2,0,1:T(4,128)S(1)} %constant_dynamic-update-slice_fusion.20), channel_id=1, source_target_pairs={{0,4},{4,8},{8,12},{12,0},{1,5},{5,9},{9,13},{13,1},{2,6},{6,10},{... | collective-permute-start | bytes 36872 | tf_op jit(solution)/shard_map/ppermute | solution.py:15
  27.3 11.4 %collective-permute-start.16 = (f32[3,4,256]{2,0,1:T(4,128)S(1)}, f32[3,4,256]{2,0,1:T(4,128)S(1)}, u32[]{:S(2)}, u32[]{:S(2)}) collective-permute-start(f32[3,4,256]{2,0,1:T(4,128)S(1)} %constant_dynamic-update-slice_fusion.20), channel_id=1, source_target_pairs={{0,8},{4,12},{8,0},{12,4},{1,9},{5,13},{9,1},{13,5},{2,10},{6,14},... | collective-permute-start | bytes 36872 | tf_op jit(solution)/shard_map/ppermute | solution.py:15
  29.0 9.7 %collective-permute-start.17 = (f32[3,4,256]{2,0,1:T(4,128)S(1)}, f32[3,4,256]{2,0,1:T(4,128)S(1)}, u32[]{:S(2)}, u32[]{:S(2)}) collective-permute-start(f32[3,4,256]{2,0,1:T(4,128)S(1)} %constant_dynamic-update-slice_fusion.20), channel_id=1, source_target_pairs={{0,12},{4,0},{8,4},{12,8},{1,13},{5,1},{9,5},{13,9},{2,14},{6,2},{... | collective-permute-start | bytes 36872 | tf_op jit(solution)/shard_map/ppermute | solution.py:15
  34.3 9.1 %collective-permute-start.3 = (f32[3,4,256]{2,0,1:T(4,128)S(1)}, f32[3,4,256]{2,0,1:T(4,128)S(1)}, u32[]{:S(2)}, u32[]{:S(2)}) collective-permute-start(f32[3,4,256]{2,0,1:T(4,128)S(1)} %constant_dynamic-update-slice_fusion.4), channel_id=1, source_target_pairs={{0,4},{4,8},{8,12},{12,0},{1,5},{5,9},{9,13},{13,1},{2,6},{6,10},{... | collective-permute-start | bytes 36872 | tf_op jit(solution)/shard_map/ppermute | solution.py:15
  34.4 12.0 %collective-permute-start.4 = (f32[3,4,256]{2,0,1:T(4,128)S(1)}, f32[3,4,256]{2,0,1:T(4,128)S(1)}, u32[]{:S(2)}, u32[]{:S(2)}) collective-permute-start(f32[3,4,256]{2,0,1:T(4,128)S(1)} %constant_dynamic-update-slice_fusion.4), channel_id=1, source_target_pairs={{0,8},{4,12},{8,0},{12,4},{1,9},{5,13},{9,1},{13,5},{2,10},{6,14},... | collective-permute-start | bytes 36872 | tf_op jit(solution)/shard_map/ppermute | solution.py:15
  35.8 10.6 %collective-permute-start.5 = (f32[3,4,256]{2,0,1:T(4,128)S(1)}, f32[3,4,256]{2,0,1:T(4,128)S(1)}, u32[]{:S(2)}, u32[]{:S(2)}) collective-permute-start(f32[3,4,256]{2,0,1:T(4,128)S(1)} %constant_dynamic-update-slice_fusion.4), channel_id=1, source_target_pairs={{0,12},{4,0},{8,4},{12,8},{1,13},{5,1},{9,5},{13,9},{2,14},{6,2},{... | collective-permute-start | bytes 36872 | tf_op jit(solution)/shard_map/ppermute | solution.py:15
  41.2 9.2 %collective-permute-start.18 = (f32[3,4,256]{2,0,1:T(4,128)S(1)}, f32[3,4,256]{2,0,1:T(4,128)S(1)}, u32[]{:S(2)}, u32[]{:S(2)}) collective-permute-start(f32[3,4,256]{2,0,1:T(4,128)S(1)} %constant_dynamic-update-slice_fusion.24), channel_id=1, source_target_pairs={{0,4},{4,8},{8,12},{12,0},{1,5},{5,9},{9,13},{13,1},{2,6},{6,10},{... | collective-permute-start | bytes 36872 | tf_op jit(solution)/shard_map/ppermute | solution.py:15
  41.8 11.4 %collective-permute-start.19 = (f32[3,4,256]{2,0,1:T(4,128)S(1)}, f32[3,4,256]{2,0,1:T(4,128)S(1)}, u32[]{:S(2)}, u32[]{:S(2)}) collective-permute-start(f32[3,4,256]{2,0,1:T(4,128)S(1)} %constant_dynamic-update-slice_fusion.24), channel_id=1, source_target_pairs={{0,8},{4,12},{8,0},{12,4},{1,9},{5,13},{9,1},{13,5},{2,10},{6,14},... | collective-permute-start | bytes 36872 | tf_op jit(solution)/shard_map/ppermute | solution.py:15
  43.5 9.7 %collective-permute-start.20 = (f32[3,4,256]{2,0,1:T(4,128)S(1)}, f32[3,4,256]{2,0,1:T(4,128)S(1)}, u32[]{:S(2)}, u32[]{:S(2)}) collective-permute-start(f32[3,4,256]{2,0,1:T(4,128)S(1)} %constant_dynamic-update-slice_fusion.24), channel_id=1, source_target_pairs={{0,12},{4,0},{8,4},{12,8},{1,13},{5,1},{9,5},{13,9},{2,14},{6,2},{... | collective-permute-start | bytes 36872 | tf_op jit(solution)/shard_map/ppermute | solution.py:15
  48.8 9.1 %collective-permute-start.6 = (f32[3,4,256]{2,0,1:T(4,128)S(1)}, f32[3,4,256]{2,0,1:T(4,128)S(1)}, u32[]{:S(2)}, u32[]{:S(2)}) collective-permute-start(f32[3,4,256]{2,0,1:T(4,128)S(1)} %constant_dynamic-update-slice_fusion.8), channel_id=1, source_target_pairs={{0,4},{4,8},{8,12},{12,0},{1,5},{5,9},{9,13},{13,1},{2,6},{6,10},{... | collective-permute-start | bytes 36872 | tf_op jit(solution)/shard_map/ppermute | solution.py:15
  48.9 12.0 %collective-permute-start.7 = (f32[3,4,256]{2,0,1:T(4,128)S(1)}, f32[3,4,256]{2,0,1:T(4,128)S(1)}, u32[]{:S(2)}, u32[]{:S(2)}) collective-permute-start(f32[3,4,256]{2,0,1:T(4,128)S(1)} %constant_dynamic-update-slice_fusion.8), channel_id=1, source_target_pairs={{0,8},{4,12},{8,0},{12,4},{1,9},{5,13},{9,1},{13,5},{2,10},{6,14},... | collective-permute-start | bytes 36872 | tf_op jit(solution)/shard_map/ppermute | solution.py:15
  50.3 10.6 %collective-permute-start.8 = (f32[3,4,256]{2,0,1:T(4,128)S(1)}, f32[3,4,256]{2,0,1:T(4,128)S(1)}, u32[]{:S(2)}, u32[]{:S(2)}) collective-permute-start(f32[3,4,256]{2,0,1:T(4,128)S(1)} %constant_dynamic-update-slice_fusion.8), channel_id=1, source_target_pairs={{0,12},{4,0},{8,4},{12,8},{1,13},{5,1},{9,5},{13,9},{2,14},{6,2},{... | collective-permute-start | bytes 36872 | tf_op jit(solution)/shard_map/ppermute | solution.py:15
  55.7 10.0 %collective-permute-start.21 = (f32[3,4,256]{2,0,1:T(4,128)S(1)}, f32[3,4,256]{2,0,1:T(4,128)S(1)}, u32[]{:S(2)}, u32[]{:S(2)}) collective-permute-start(f32[3,4,256]{2,0,1:T(4,128)S(1)} %constant_dynamic-update-slice_fusion.28), channel_id=1, source_target_pairs={{0,4},{4,8},{8,12},{12,0},{1,5},{5,9},{9,13},{13,1},{2,6},{6,10},{... | collective-permute-start | bytes 36872 | tf_op jit(solution)/shard_map/ppermute | solution.py:15
  56.3 10.6 %collective-permute-start.22 = (f32[3,4,256]{2,0,1:T(4,128)S(1)}, f32[3,4,256]{2,0,1:T(4,128)S(1)}, u32[]{:S(2)}, u32[]{:S(2)}) collective-permute-start(f32[3,4,256]{2,0,1:T(4,128)S(1)} %constant_dynamic-update-slice_fusion.28), channel_id=1, source_target_pairs={{0,8},{4,12},{8,0},{12,4},{1,9},{5,13},{9,1},{13,5},{2,10},{6,14},... | collective-permute-start | bytes 36872 | tf_op jit(solution)/shard_map/ppermute | solution.py:15
  58.0 8.9 %collective-permute-start.23 = (f32[3,4,256]{2,0,1:T(4,128)S(1)}, f32[3,4,256]{2,0,1:T(4,128)S(1)}, u32[]{:S(2)}, u32[]{:S(2)}) collective-permute-start(f32[3,4,256]{2,0,1:T(4,128)S(1)} %constant_dynamic-update-slice_fusion.28), channel_id=1, source_target_pairs={{0,12},{4,0},{8,4},{12,8},{1,13},{5,1},{9,5},{13,9},{2,14},{6,2},{... | collective-permute-start | bytes 36872 | tf_op jit(solution)/shard_map/ppermute | solution.py:15
  63.3 24.3 %collective-permute-start.10 = (f32[3,4,256]{2,0,1:T(4,128)S(1)}, f32[3,4,256]{2,0,1:T(4,128)S(1)}, u32[]{:S(2)}, u32[]{:S(2)}) collective-permute-start(f32[3,4,256]{2,0,1:T(4,128)S(1)} %constant_dynamic-update-slice_fusion.12), channel_id=1, source_target_pairs={{0,8},{4,12},{8,0},{12,4},{1,9},{5,13},{9,1},{13,5},{2,10},{6,14},... | collective-permute-start | bytes 36872 | tf_op jit(solution)/shard_map/ppermute | solution.py:15
  64.3 23.3 %collective-permute-start.11 = (f32[3,4,256]{2,0,1:T(4,128)S(1)}, f32[3,4,256]{2,0,1:T(4,128)S(1)}, u32[]{:S(2)}, u32[]{:S(2)}) collective-permute-start(f32[3,4,256]{2,0,1:T(4,128)S(1)} %constant_dynamic-update-slice_fusion.12), channel_id=1, source_target_pairs={{0,12},{4,0},{8,4},{12,8},{1,13},{5,1},{9,5},{13,9},{2,14},{6,2},{... | collective-permute-start | bytes 36872 | tf_op jit(solution)/shard_map/ppermute | solution.py:15
  65.7 21.9 %collective-permute-start.9 = (f32[3,4,256]{2,0,1:T(4,128)S(1)}, f32[3,4,256]{2,0,1:T(4,128)S(1)}, u32[]{:S(2)}, u32[]{:S(2)}) collective-permute-start(f32[3,4,256]{2,0,1:T(4,128)S(1)} %constant_dynamic-update-slice_fusion.12), channel_id=1, source_target_pairs={{0,4},{4,8},{8,12},{12,0},{1,5},{5,9},{9,13},{13,1},{2,6},{6,10},{... | collective-permute-start | bytes 36872 | tf_op jit(solution)/shard_map/ppermute | solution.py:15
  (4 other events, 23.0 us)
where the time goes:
time: 90.1 us; the launch traced here: 89.9 us
  starting transfers between devices  36.9 us (41%)
  blocking collectives  23.9 us (27%)
  local copies, waits for them, and re-layouts  22.3 us (25%)
  matrix products  2.63 us (3%)
  other arithmetic  2.6 us (3%)
  between operations  1.55 us (2%)
    ppermute x24, starting transfers between devices, from_behind(): return lax.ppermute(value, axis, pairs)  36.9 us
    psum x1, blocking collectives, tile_total(): return lax.psum(filter_part, 'tile')  18.3 us
    all_gather x1, blocking collectives, on_device(): whole_grad = lax.all_gather(out_grad, 'sub', axis=1, tiled=True)  5.58 us
    gather x8, local copies, waits for them, and re-layouts, laplace(): ghosts = stacked[local_rows, my_edges]  4.87 us
    another operation x40, local copies, waits for them, and re-layouts, edge_lines(): jnp.stack([values[..., :tile_side], values[..., -tile_side:], values[...,...  2.57 us
  transfers between devices with their start and end apart: 24, of which 0 were waited for; matrix products, arithmetic and copies ran while one was open for 26% of the time, Pallas kernels for 0%

commit v1 on v0

--- a/solution.py
+++ b/solution.py
@@ -1,9 +1,12 @@
+import functools
 import math
 
 import jax
 import jax.numpy as jnp
 import numpy as np
 from jax import lax
+from jax.experimental import pallas as pl
+from jax.experimental.pallas import tpu as pltpu
 from jax.sharding import PartitionSpec as P
 
 K = 5
@@ -155,7 +158,7 @@
     return lax.psum(filter_part, "tile")
 
 
-def on_device(features, out_grad, filters, tile_map):
+def general_path(features, out_grad, filters, tile_map):
     slot_count = features.shape[0]
     group_channels = features.shape[1]
     tile_side = math.isqrt(features.shape[2])
@@ -210,6 +213,420 @@
     return (in_grad, weight_grad)
 
 
+DEPTH = K - 1
+GHOST_SIDES = (0, 2, 3, 1)
+
+
+def face_graph(tile_side):
+    tile_ids = np.arange(12, dtype=np.int64)
+    target_list, edge_list = neighbour_codes(tile_ids, 1, 1)
+    targets = np.stack(target_list, axis=1)
+    edges = np.stack(edge_list, axis=1)
+    pixels = tile_side * tile_side
+    grid = np.arange(pixels).reshape(tile_side, tile_side)
+    lines = [grid[0], grid[-1], grid[:, 0], grid[:, -1]]
+    ghosts = np.zeros((12, 4, tile_side), dtype=np.int64)
+    around = np.zeros((12, 4, tile_side, tile_side), dtype=np.int64)
+    for tile in range(12):
+        for side in range(4):
+            ghosts[tile, side] = targets[tile, side] * pixels + lines[edges[tile, side]]
+        whole = tile * pixels + grid
+        around[tile, 0] = np.concatenate([ghosts[tile, 0][None], whole[:-1]], 0)
+        around[tile, 1] = np.concatenate([whole[1:], ghosts[tile, 1][None]], 0)
+        around[tile, 2] = np.concatenate([ghosts[tile, 2][:, None], whole[:, :-1]], 1)
+        around[tile, 3] = np.concatenate([whole[:, 1:], ghosts[tile, 3][:, None]], 1)
+    around = around.transpose(0, 2, 3, 1).reshape(12 * pixels, 4)
+    return targets, edges, ghosts, around
+
+
+@functools.lru_cache(None)
+def ghost_tables(tile_side):
+    targets, edges, ghosts, around = face_graph(tile_side)
+    pixels = tile_side * tile_side
+    grid = np.arange(pixels).reshape(tile_side, tile_side)
+    strips = np.stack(
+        [
+            grid[:DEPTH].ravel(),
+            grid[-DEPTH:].ravel(),
+            grid[:, :DEPTH].T.ravel(),
+            grid[:, -DEPTH:].T.ravel(),
+        ]
+    )
+    table = np.zeros((12, 10), dtype=np.int32)
+    by_class = []
+    for tile in range(12):
+        wanted = np.concatenate([ghosts[tile, side] for side in GHOST_SIDES])
+        power = np.zeros((wanted.size, 12 * pixels), dtype=np.int32)
+        power[np.arange(wanted.size), wanted] = 1
+        powers = [power]
+        for _ in range(DEPTH - 1):
+            powers.append(sum(powers[-1][:, around[:, side]] for side in range(4)))
+        rows = np.concatenate(
+            [powers[0], powers[1], powers[2] - 8 * powers[0], powers[3] - 12 * powers[1]]
+        )
+        support = np.flatnonzero(np.any(rows != 0, axis=0))
+        sources = [(int(targets[tile, side]), int(edges[tile, side])) for side in range(4)]
+        sources += [(tile, side) for side in range(4)]
+        covered = set(int(t) * pixels + int(p) for t, e in sources for p in strips[e])
+        left = [int(p) for p in support if int(p) not in covered]
+        corner_tiles = {}
+        for pixel in left:
+            corner_tiles.setdefault(pixel // pixels, []).append(pixel % pixels)
+        first = lambda t: int(
+            np.flatnonzero(np.any(rows[:, [t * pixels + p for p in corner_tiles[t]]] != 0, axis=1))[0]
+        )
+        for other in sorted(corner_tiles, key=first):
+            choice = [e for e in range(4) if set(corner_tiles[other]) <= set(strips[e].tolist())]
+            sources.append((other, choice[0]))
+        assert len(sources) <= 10
+        while len(sources) < 10:
+            sources.append(sources[-1])
+        table[tile] = [t * 4 + e for t, e in sources]
+        lanes = np.concatenate([t * pixels + strips[e] for t, e in sources])
+        seen, keep = set(), np.zeros(lanes.size, dtype=bool)
+        for lane, pixel in enumerate(lanes.tolist()):
+            keep[lane] = pixel not in seen
+            seen.add(pixel)
+        assert set(support.tolist()) <= seen
+        matrix = (rows[:, lanes] * keep[None]).T
+        assert np.abs(matrix).max() <= 127
+        if tile % 4 == 0:
+            by_class.append(matrix)
+        else:
+            assert np.array_equal(matrix, by_class[-1])
+    spread = np.zeros((4, tile_side, tile_side, tile_side), dtype=np.float32)
+    step = np.arange(tile_side)
+    spread[0, step, 0, step] = 1
+    spread[1, step, step, 0] = 1
+    spread[2, step, step, -1] = 1
+    spread[3, step, -1, step] = 1
+    spread = spread.reshape(4 * tile_side, pixels)
+    take = np.zeros((pixels, 2 * DEPTH * tile_side), dtype=np.float32)
+    take[np.concatenate([strips[2], strips[3]]), np.arange(2 * DEPTH * tile_side)] = 1
+    return np.stack(by_class).astype(np.int8), table.reshape(-1), spread, take
+
+
+def face_kernel(
+    sizes,
+    x_ref,
+    g_ref,
+    f_ref,
+    map_ref,
+    table_ref,
+    ghost_hbm,
+    spread_hbm,
+    take_hbm,
+    in_ref,
+    w_ref,
+    strips,
+    x_all,
+    part,
+    part_in,
+    block,
+    block_in,
+    ghost_raw,
+    ghost,
+    spread,
+    take,
+    load_sem,
+    s_send,
+    s_recv,
+    x_send,
+    x_recv,
+    p_send,
+    p_recv,
+    w_send,
+    w_recv,
+):
+    slots, tiles_n, subs, side, scale = sizes
+    chans = x_ref.shape[1]
+    pixels = side * side
+    width = DEPTH * side
+    j = lax.axis_index("tile")
+    s = lax.axis_index("sub")
+    tile_peers = [lax.rem(j + d, tiles_n) for d in range(1, tiles_n)]
+    sub_peers = [lax.rem(s + d, subs) for d in range(1, subs)]
+    every = [(d, e) for d in range(tiles_n) for e in range(subs) if d + e > 0]
+
+    def device(d, e):
+        return {"tile": lax.rem(j + d, tiles_n), "sub": lax.rem(s + e, subs)}
+
+    barrier = pltpu.get_barrier_semaphore()
+    for d, e in every:
+        pl.semaphore_signal(
+            barrier, inc=1, device_id=device(d, e), device_id_type=pl.DeviceIdType.MESH
+        )
+    loads = [
+        pltpu.make_async_copy(take_hbm, take, load_sem.at[0]),
+        pltpu.make_async_copy(spread_hbm, spread, load_sem.at[1]),
+    ]
+    for m in range(slots):
+        kind = (slots * j + m) // 4
+        loads.append(
+            pltpu.make_async_copy(ghost_hbm.at[kind], ghost_raw.at[m], load_sem.at[2 + m])
+        )
+    for copy in loads:
+        copy.start()
+
+    base = slots * j
+
+    def slot_of(m):
+        found = 0
+        for slot in range(1, slots):
+            found = jnp.where(map_ref[base + slot] == base + m, slot, found)
+        return found
+
+    slot_list = [slot_of(m) for m in range(slots)]
+    own = [g_ref[slot_list[m]].astype(jnp.float32) for m in range(slots)]
+    stacked = jnp.concatenate(own, axis=0).astype(jnp.bfloat16)
+    loads[0].wait()
+    cut = jnp.dot(stacked, take[...], preferred_element_type=jnp.float32)
+    for m in range(slots):
+        rows = slice(m * chans, (m + 1) * chans)
+        row = (base + m) * 4
+        strips[row] = own[m][:, :width].astype(jnp.bfloat16)
+        strips[row + 1] = own[m][:, pixels - width :].astype(jnp.bfloat16)
+        strips[row + 2] = cut[rows, :width].astype(jnp.bfloat16)
+        strips[row + 3] = cut[rows, width:].astype(jnp.bfloat16)
+    pl.semaphore_wait(barrier, len(every))
+
+    def strip_copy(d, sender, target):
+        mine = strips.at[pl.ds(sender * slots * 4, slots * 4)]
+        return pltpu.make_async_remote_copy(
+            mine,
+            mine,
+            s_send.at[d],
+            s_recv.at[sender],
+            device_id={"tile": target},
+            device_id_type=pl.DeviceIdType.MESH,
+        )
+
+    def x_copy(d, sender, target):
+        return pltpu.make_async_remote_copy(
+            x_ref,
+            x_all.at[sender],
+            x_send.at[d],
+            x_recv.at[sender],
+            device_id={"sub": target},
+            device_id_type=pl.DeviceIdType.MESH,
+        )
+
+    def part_copy(m, d, sender, target):
+        return pltpu.make_async_remote_copy(
+            part.at[m, target],
+            part_in.at[m, sender],
+            p_send.at[m, d],
+            p_recv.at[m, sender],
+            device_id={"sub": target},
+            device_id_type=pl.DeviceIdType.MESH,
+        )
+
+    def block_copy(order, d, e, sender):
+        return pltpu.make_async_remote_copy(
+            block.at[lax.rem(s + e, subs)],
+            block_in.at[sender],
+            w_send.at[order],
+            w_recv.at[sender],
+            device_id=device(d, e),
+            device_id_type=pl.DeviceIdType.MESH,
+        )
+
+    for d, peer in enumerate(tile_peers):
+        strip_copy(d, j, peer).start()
+    for d, peer in enumerate(sub_peers):
+        x_copy(d, s, peer).start()
+
+    total_rows = (2 * K - 1) * chans
+    row_k = lax.broadcasted_iota(jnp.int32, (subs * chans, total_rows), 1) // chans
+    row_o = lax.broadcasted_iota(jnp.int32, (subs * chans, total_rows), 1) % chans
+    from_o = lax.broadcasted_iota(jnp.int32, (subs * chans, total_rows), 0)
+    mine_o = from_o == row_o + chans * s
+    mixing = jnp.zeros((subs * chans, total_rows), jnp.float32)
+    for k in range(K):
+        chosen = jnp.where(mine_o & ((row_k + 1) // 2 == k), 1.0, 0.0).astype(jnp.bfloat16)
+        mixing = mixing + jnp.dot(f_ref[k], chosen, preferred_element_type=jnp.float32)
+    mixing = mixing.astype(jnp.bfloat16)
+
+    for copy in loads[1:]:
+        copy.wait()
+    chunk = 128
+
+    def widen(step, carry):
+        at = pl.ds(pl.multiple_of(step * chunk, chunk), chunk)
+        for m in range(slots):
+            ghost[m, at, :] = ghost_raw[m, at, :].astype(jnp.float32).astype(jnp.bfloat16)
+        return carry
+
+    lax.fori_loop(0, ghost.shape[1] // chunk, widen, 0)
+
+    for d, peer in enumerate(tile_peers):
+        strip_copy(d, peer, peer).wait_recv()
+    lane = lax.broadcasted_iota(jnp.int32, (chans, pixels), 1)
+    y_at = lane % side
+    scales = (1.0, -0.25, 0.125, -0.0625)
+    grad = jnp.zeros((subs * chans, total_rows), jnp.float32)
+    terms = []
+    for m in range(slots):
+        pieces = [
+            strips[table_ref[(base + m) * 10 + r]].astype(jnp.float32) for r in range(10)
+        ]
+        source = jnp.concatenate(pieces, axis=1).astype(jnp.bfloat16)
+        lines = jnp.dot(source, ghost[m], preferred_element_type=jnp.float32)
+        lines = jnp.concatenate(
+            [lines[:, k * 4 * side : (k + 1) * 4 * side] * scales[k] for k in range(DEPTH)], axis=0
+        )
+        high = lines.astype(jnp.bfloat16).astype(jnp.float32)
+        rest = lines - high
+        middle = rest.astype(jnp.bfloat16).astype(jnp.float32)
+        split = jnp.concatenate([high, middle, rest - middle], axis=0).astype(jnp.bfloat16)
+        outer = jnp.dot(split, spread[...], preferred_element_type=jnp.float32)
+        count = DEPTH * chans
+        outer = outer[:count] + outer[count : 2 * count] + outer[2 * count :]
+
+        def around(value, k):
+            total = outer[k * chans : (k + 1) * chans]
+            total = total + jnp.where(lane < side, 0.0, pltpu.roll(value, side, 1))
+            total = total + jnp.where(
+                lane >= pixels - side, 0.0, pltpu.roll(value, pixels - side, 1)
+            )
+            total = total + jnp.where(y_at == 0, 0.0, pltpu.roll(value, 1, 1))
+            return total + jnp.where(y_at == side - 1, 0.0, pltpu.roll(value, pixels - 1, 1))
+
+        previous, current = own[m], -0.25 * around(own[m], 0)
+        held = [previous]
+        for k in range(1, K):
+            high = current.astype(jnp.bfloat16).astype(jnp.float32)
+            held += [high, current - high]
+            if k < K - 1:
+                previous, current = current, -0.5 * around(current, k) - previous
+        term = jnp.concatenate(held, axis=0).astype(jnp.bfloat16)
+        terms.append(term)
+        mixed = jnp.dot(mixing, term, preferred_element_type=jnp.float32)
+        for e in range(subs):
+            part[m, e] = mixed[e * chans : (e + 1) * chans]
+        for d, peer in enumerate(sub_peers):
+            part_copy(m, d, s, peer).start()
+
+    x_all[s] = x_ref[...]
+    for d, peer in enumerate(sub_peers):
+        x_copy(d, peer, peer).wait_recv()
+    for m in range(slots):
+        maps = jnp.concatenate(
+            [x_all[e, slot_list[m]].astype(jnp.float32) for e in range(subs)], axis=0
+        ).astype(jnp.bfloat16)
+        grad = grad + lax.dot_general(
+            maps, terms[m], (((1,), (1,)), ((), ())), preferred_element_type=jnp.float32
+        )
+    sums = [grad[:, :chans]]
+    for k in range(1, K):
+        at = (2 * k - 1) * chans
+        sums.append(grad[:, at : at + chans] + grad[:, at + chans : at + 2 * chans])
+    sums.append(jnp.zeros((subs * chans, block.shape[2] - K * chans), jnp.float32))
+    blocks = jnp.concatenate(sums, axis=1) * scale
+    for e in range(subs):
+        block[e] = blocks[e * chans : (e + 1) * chans]
+    me = j * subs + s
+    for order, (d, e) in enumerate(every):
+        block_copy(order, d, e, me).start()
+    block_in[me] = block[s]
+
+    for m in range(slots):
+        for d, peer in enumerate(sub_peers):
+            part_copy(m, d, peer, peer).wait_recv()
+        part_in[m, s] = part[m, s]
+    for slot in range(slots):
+        m = lax.rem(map_ref[base + slot], slots)
+        total = part_in[m, 0]
+        for e in range(1, subs):
+            total = total + part_in[m, e]
+        in_ref[slot] = total.astype(in_ref.dtype)
+
+    for order, (d, e) in enumerate(every):
+        sender = lax.rem(j + d, tiles_n) * subs + lax.rem(s + e, subs)
+        block_copy(order, d, e, sender).wait_recv()
+    whole = []
+    for e in range(subs):
+        total = block_in[e]
+        for t in range(1, tiles_n):
+            total = total + block_in[t * subs + e]
+        whole.append(total)
+    for k in range(K):
+        w_ref[k] = jnp.concatenate([v[:, k * chans : (k + 1) * chans] for v in whole], axis=1)
+
+    for d, peer in enumerate(tile_peers):
+        strip_copy(d, j, peer).wait_send()
+    for d, peer in enumerate(sub_peers):
+        x_copy(d, s, peer).wait_send()
+        for m in range(slots):
+            part_copy(m, d, s, peer).wait_send()
+    for order, (d, e) in enumerate(every):
+        block_copy(order, d, e, me).wait_send()
+
+
+def face_path(features, out_grad, filters, tile_map):
+    slots, chans, pixels = features.shape
+    side = math.isqrt(pixels)
+    tiles_n, subs = lax.axis_size("tile"), lax.axis_size("sub")
+    matrices, table, spread, take = ghost_tables(side)
+    scale = 1.0 / math.sqrt(slots * tiles_n * pixels)
+    width = DEPTH * side
+    vmem = pl.BlockSpec(memory_space=pltpu.VMEM)
+    smem = pl.BlockSpec(memory_space=pltpu.SMEM)
+    hbm = pl.BlockSpec(memory_space=pl.ANY)
+    dma = pltpu.SemaphoreType.DMA
+    return pl.pallas_call(
+        functools.partial(face_kernel, (slots, tiles_n, subs, side, scale)),
+        out_shape=(
+            jax.ShapeDtypeStruct(features.shape, jnp.bfloat16),
+            jax.ShapeDtypeStruct((K, chans, filters.shape[2]), jnp.float32),
+        ),
+        in_specs=[vmem, vmem, vmem, smem, smem, hbm, hbm, hbm],
+        out_specs=(vmem, vmem),
+        scratch_shapes=[
+            pltpu.VMEM((slots * tiles_n * 4, chans, width), jnp.bfloat16),
+            pltpu.VMEM((subs,) + features.shape, jnp.bfloat16),
+            pltpu.VMEM((slots, subs, chans, pixels), jnp.float32),
+            pltpu.VMEM((slots, subs, chans, pixels), jnp.float32),
+            pltpu.VMEM((subs, chans, 128), jnp.float32),
+            pltpu.VMEM((subs * tiles_n, chans, 128), jnp.float32),
+            pltpu.VMEM((slots,) + matrices.shape[1:], jnp.int8),
+            pltpu.VMEM((slots,) + matrices.shape[1:], jnp.bfloat16),
+            pltpu.VMEM(spread.shape, jnp.bfloat16),
+            pltpu.VMEM(take.shape, jnp.bfloat16),
+            dma((2 + slots,)),
+            dma((tiles_n,)),
+            dma((tiles_n,)),
+            dma((subs,)),
+            dma((subs,)),
+            dma((slots, subs)),
+            dma((slots, subs)),
+            dma((subs * tiles_n,)),
+            dma((subs * tiles_n,)),
+        ],
+        compiler_params=pltpu.CompilerParams(
+            collective_id=0, has_side_effects=True, vmem_limit_bytes=40 * 2**20
+        ),
+    )(
+        features,
+        out_grad,
+        filters,
+        tile_map,
+        jnp.asarray(table),
+        jnp.asarray(matrices),
+        jnp.asarray(spread, jnp.bfloat16),
+        jnp.asarray(take, jnp.bfloat16),
+    )
+
+
+def on_device(features, out_grad, filters, tile_map):
+    slots, chans, pixels = features.shape
+    side = math.isqrt(pixels)
+    whole_faces = slots * lax.axis_size("tile") == 12
+    if whole_faces and DEPTH * side == 128 and chans % 8 == 0 and K * chans <= 128:
+        return face_path(features, out_grad, filters, tile_map)
+    return general_path(features, out_grad, filters, tile_map)
+
+
 def solution(mesh):
     placed = (P(("grp", "tile"), "sub", None), P(("grp", "tile"), "sub", None), P(), P())
     return jax.shard_map(

time: 90.1 us -> 28.3 us (0.31)
  starting transfers between devices: 36.9 us -> 0 us
  blocking collectives: 23.9 us -> 0 us
  Pallas kernels: 0 us -> 18.8 us
  local copies, waits for them, and re-layouts: 22.3 us -> 8.44 us
  matrix products: 2.63 us -> 0 us
  other arithmetic: 2.6 us -> 0 us
    ppermute x24 -> x0, starting transfers between devices: 36.9 us -> none  [from_behind(): return lax.ppermute(value, axis, pairs)]
    pallas_call x0 -> x1, Pallas kernels: none -> 18.8 us  [face_path(): pl.pallas_call(functools.partial(face_kernel, (slots, tiles_n, subs, side...]
    psum x1 -> x0, blocking collectives: 18.3 us -> none  [tile_total(): return lax.psum(filter_part, 'tile')]
    unnamed x33 -> x18, local copies, waits for them, and re-layouts: 0.84 us -> 8.44 us
    gather x11 -> x0, local copies, waits for them, and re-layouts: 6.38 us -> none  [the longest x8 4.87 us: laplace(): ghosts = stacked[local_rows, my_edges]]
    all_gather x1 -> x0, blocking collectives: 5.58 us -> none  [on_device(): whole_grad = lax.all_gather(out_grad, 'sub', axis=1, tiled=True)]
    slice x40 -> x0, local copies, waits for them, and re-layouts: 5.42 us -> none  [the longest x8 1.34 us: edge_lines(): values[..., -tile_side:]]
    reshape x24 -> x0, local copies, waits for them, and re-layouts: 3.72 us -> none  [the longest x8 1.41 us: stencil(): jnp.repeat(ghosts[:, 3], tile_side, axis=-1)]
  transfers between devices with their start and end apart: 24 -> 0, of which waited for: 0 -> 0; matrix products, arithmetic and copies ran while one was open for 26% -> 0% of each run, Pallas kernels for 0% -> 0%
where the time goes in v1:
time: 28.3 us; the launch traced here: 27.8 us
  Pallas kernels  18.8 us (66%)
  local copies, waits for them, and re-layouts  8.44 us (30%)
  between operations  0.65 us (2%)
    pallas_call x1, Pallas kernels, face_path(): pl.pallas_call(functools.partial(face_kernel, (slots, tiles_n, subs, side...  18.8 us
    unnamed x18, local copies, waits for them, and re-layouts  8.44 us

profile of v1, /device:TPU:0, one launch (start us, length us, event | category | flops | bytes accessed | tf_op | source)
XLA Modules:
  0.0 27.8 jit_solution(12424714745513141825)
XLA Ops:
  0.6 0.0 copy-start
  0.6 1.5 %copy-done = s8[3,1280,512]{2,1,0:T(32,128)(4,1)S(1)} copy-done((s8[3,1280,512]{2,1,0:T(32,128)(4,1)S(1)}, s8[3,1280,512]{2,1,0:T(32,128)(4,1)}, u32[]{:S(2)}) %copy-start) | copy-done | bytes 1966104
  2.2 0.0 copy-start.1
  2.2 1.0 %copy-done.1 = bf16[1024,256]{1,0:T(8,128)(2,1)S(1)} copy-done((bf16[1024,256]{1,0:T(8,128)(2,1)S(1)}, bf16[1024,256]{1,0:T(8,128)(2,1)}, u32[]{:S(2)}) %copy-start.1) | copy-done | bytes 524312
  3.2 0.0 copy-start.2
  3.2 0.9 %copy-done.2 = bf16[128,1024]{1,0:T(8,128)(2,1)S(1)} copy-done((bf16[128,1024]{1,0:T(8,128)(2,1)S(1)}, bf16[128,1024]{1,0:T(8,128)(2,1)}, u32[]{:S(2)}) %copy-start.2) | copy-done | bytes 262168
  4.2 0.0 copy-start.3
  4.2 0.8 %copy-done.3 = bf16[3,8,1024]{2,1,0:T(8,128)(2,1)S(1)} copy-done((bf16[3,8,1024]{2,1,0:T(8,128)(2,1)S(1)}, bf16[3,8,1024]{2,1,0:T(8,128)(2,1)}, u32[]{:S(2)}) %copy-start.3) | copy-done | bytes 49176
  5.0 0.0 copy-start.4
  5.0 0.8 %copy-done.4 = bf16[3,8,1024]{2,1,0:T(8,128)(2,1)S(1)} copy-done((bf16[3,8,1024]{2,1,0:T(8,128)(2,1)S(1)}, bf16[3,8,1024]{2,1,0:T(8,128)(2,1)}, u32[]{:S(2)}) %copy-start.4) | copy-done | bytes 49176
  5.8 0.0 copy-start.5
  5.8 0.8 %copy-done.5 = bf16[5,32,32]{2,1,0:T(8,128)(2,1)S(1)} copy-done((bf16[5,32,32]{2,1,0:T(8,128)(2,1)S(1)}, bf16[5,32,32]{2,1,0:T(8,128)(2,1)}, u32[]{:S(2)}) %copy-start.5) | copy-done | bytes 10264
  6.5 0.0 copy-start.6
  6.6 0.7 %copy-done.6 = s32[12]{0:T(128)S(1)} copy-done((s32[12]{0:T(128)S(1)}, s32[12]{0:T(128)}, u32[]{:S(2)}) %copy-start.6) | copy-done | bytes 72
  7.2 0.0 copy-start.7
  7.2 0.7 %copy-done.7 = s32[120]{0:T(128)S(1)} copy-done((s32[120]{0:T(128)S(1)}, s32[120]{0:T(128)}, u32[]{:S(2)}) %copy-start.7) | copy-done | bytes 504
  7.9 18.8 %shard_map.95 = (bf16[3,8,1024]{2,1,0:T(8,128)(2,1)S(1)}, f32[5,8,32]{2,1,0:T(8,128)S(1)}) custom-call(bf16[3,8,1024]{2,1,0:T(8,128)(2,1)S(1)} %copy-done.3, bf16[3,8,1024]{2,1,0:T(8,128)(2,1)S(1)} %copy-done.4, bf16[5,32,32]{2,1,0:T(8,128)(2,1)S(1)} %copy-done.5, s32[12]{0:T(128)S(1)} %copy-done.6, s32[120]{0:T(128)S(1)} %copy-done.7, ...), custom_call_target="tpu_custom_call" | custom-call | tf_op jit(solution)/shard_map/pallas_call | solution.py:577
  26.6 0.6 %copy.12 = bf16[3,8,1024]{2,1,0:T(8,128)(2,1)} copy(bf16[3,8,1024]{2,1,0:T(8,128)(2,1)S(1)} %get-tuple-element.4) | data formatting | bytes 98304
  27.2 0.6 %copy.13 = f32[5,8,32]{2,1,0:T(8,128)} copy(f32[5,8,32]{2,1,0:T(8,128)S(1)} %get-tuple-element.5) | data formatting | bytes 10240
Async XLA Ops:
  0.6 1.5 %copy-start = (s8[3,1280,512]{2,1,0:T(32,128)(4,1)S(1)}, s8[3,1280,512]{2,1,0:T(32,128)(4,1)}, u32[]{:S(2)}) copy-start(s8[3,1280,512]{2,1,0:T(32,128)(4,1)} %constant.9.clone.ghost_hbm) | copy-start | bytes 5898244
  2.2 1.0 %copy-start.1 = (bf16[1024,256]{1,0:T(8,128)(2,1)S(1)}, bf16[1024,256]{1,0:T(8,128)(2,1)}, u32[]{:S(2)}) copy-start(bf16[1024,256]{1,0:T(8,128)(2,1)} %constant.11.clone.take_hbm) | copy-start | bytes 1572868
  3.2 0.9 %copy-start.2 = (bf16[128,1024]{1,0:T(8,128)(2,1)S(1)}, bf16[128,1024]{1,0:T(8,128)(2,1)}, u32[]{:S(2)}) copy-start(bf16[128,1024]{1,0:T(8,128)(2,1)} %constant.10.clone.spread_hbm) | copy-start | bytes 786436
  4.2 0.8 %copy-start.3 = (bf16[3,8,1024]{2,1,0:T(8,128)(2,1)S(1)}, bf16[3,8,1024]{2,1,0:T(8,128)(2,1)}, u32[]{:S(2)}) copy-start(bf16[3,8,1024]{2,1,0:T(8,128)(2,1)} %x_ref.1) | copy-start | bytes 147460
  5.0 0.8 %copy-start.4 = (bf16[3,8,1024]{2,1,0:T(8,128)(2,1)S(1)}, bf16[3,8,1024]{2,1,0:T(8,128)(2,1)}, u32[]{:S(2)}) copy-start(bf16[3,8,1024]{2,1,0:T(8,128)(2,1)} %g_ref.1) | copy-start | bytes 147460
  5.8 0.8 %copy-start.5 = (bf16[5,32,32]{2,1,0:T(8,128)(2,1)S(1)}, bf16[5,32,32]{2,1,0:T(8,128)(2,1)}, u32[]{:S(2)}) copy-start(bf16[5,32,32]{2,1,0:T(8,128)(2,1)} %f_ref.1) | copy-start | bytes 30724
  6.5 0.7 %copy-start.6 = (s32[12]{0:T(128)S(1)}, s32[12]{0:T(128)}, u32[]{:S(2)}) copy-start(s32[12]{0:T(128)} %map_ref.1) | copy-start | bytes 148
  7.2 0.7 %copy-start.7 = (s32[120]{0:T(128)S(1)}, s32[120]{0:T(128)}, u32[]{:S(2)}) copy-start(s32[120]{0:T(128)} %constant.8.clone.table_ref) | copy-start | bytes 1444

commit v2 on v1

--- a/solution.py
+++ b/solution.py
@@ -308,11 +308,11 @@
 
 def face_kernel(
     sizes,
-    x_ref,
-    g_ref,
-    f_ref,
-    map_ref,
-    table_ref,
+    x_hbm,
+    g_hbm,
+    f_hbm,
+    map_hbm,
+    table_hbm,
     ghost_hbm,
     spread_hbm,
     take_hbm,
@@ -328,6 +328,10 @@
     ghost,
     spread,
     take,
+    g_ref,
+    f_ref,
+    map_ref,
+    table_ref,
     load_sem,
     s_send,
     s_recv,
@@ -339,7 +343,7 @@
     w_recv,
 ):
     slots, tiles_n, subs, side, scale = sizes
-    chans = x_ref.shape[1]
+    chans = g_ref.shape[1]
     pixels = side * side
     width = DEPTH * side
     j = lax.axis_index("tile")
@@ -351,24 +355,35 @@
     def device(d, e):
         return {"tile": lax.rem(j + d, tiles_n), "sub": lax.rem(s + e, subs)}
 
+    slot_loads = [
+        pltpu.make_async_copy(map_hbm, map_ref, load_sem.at[0]),
+        pltpu.make_async_copy(g_hbm, g_ref, load_sem.at[1]),
+        pltpu.make_async_copy(take_hbm, take, load_sem.at[2]),
+    ]
+    for copy in slot_loads:
+        copy.start()
     barrier = pltpu.get_barrier_semaphore()
     for d, e in every:
         pl.semaphore_signal(
             barrier, inc=1, device_id=device(d, e), device_id_type=pl.DeviceIdType.MESH
         )
     loads = [
-        pltpu.make_async_copy(take_hbm, take, load_sem.at[0]),
-        pltpu.make_async_copy(spread_hbm, spread, load_sem.at[1]),
+        pltpu.make_async_copy(f_hbm, f_ref, load_sem.at[3]),
+        pltpu.make_async_copy(table_hbm, table_ref, load_sem.at[4]),
+        pltpu.make_async_copy(spread_hbm, spread, load_sem.at[5]),
+        pltpu.make_async_copy(x_hbm, x_all.at[s], load_sem.at[6]),
     ]
     for m in range(slots):
         kind = (slots * j + m) // 4
         loads.append(
-            pltpu.make_async_copy(ghost_hbm.at[kind], ghost_raw.at[m], load_sem.at[2 + m])
+            pltpu.make_async_copy(ghost_hbm.at[kind], ghost_raw.at[m], load_sem.at[7 + m])
         )
     for copy in loads:
         copy.start()
 
     base = slots * j
+    for copy in slot_loads:
+        copy.wait()
 
     def slot_of(m):
         found = 0
@@ -379,7 +394,6 @@
     slot_list = [slot_of(m) for m in range(slots)]
     own = [g_ref[slot_list[m]].astype(jnp.float32) for m in range(slots)]
     stacked = jnp.concatenate(own, axis=0).astype(jnp.bfloat16)
-    loads[0].wait()
     cut = jnp.dot(stacked, take[...], preferred_element_type=jnp.float32)
     for m in range(slots):
         rows = slice(m * chans, (m + 1) * chans)
@@ -403,7 +417,7 @@
 
     def x_copy(d, sender, target):
         return pltpu.make_async_remote_copy(
-            x_ref,
+            x_hbm,
             x_all.at[sender],
             x_send.at[d],
             x_recv.at[sender],
@@ -436,6 +450,7 @@
     for d, peer in enumerate(sub_peers):
         x_copy(d, s, peer).start()
 
+    loads[0].wait()
     total_rows = (2 * K - 1) * chans
     row_k = lax.broadcasted_iota(jnp.int32, (subs * chans, total_rows), 1) // chans
     row_o = lax.broadcasted_iota(jnp.int32, (subs * chans, total_rows), 1) % chans
@@ -507,7 +522,6 @@
         for d, peer in enumerate(sub_peers):
             part_copy(m, d, s, peer).start()
 
-    x_all[s] = x_ref[...]
     for d, peer in enumerate(sub_peers):
         x_copy(d, peer, peer).wait_recv()
     for m in range(slots):
@@ -571,8 +585,7 @@
     scale = 1.0 / math.sqrt(slots * tiles_n * pixels)
     width = DEPTH * side
     vmem = pl.BlockSpec(memory_space=pltpu.VMEM)
-    smem = pl.BlockSpec(memory_space=pltpu.SMEM)
-    hbm = pl.BlockSpec(memory_space=pl.ANY)
+    hbm = pl.BlockSpec(memory_space=pltpu.HBM)
     dma = pltpu.SemaphoreType.DMA
     return pl.pallas_call(
         functools.partial(face_kernel, (slots, tiles_n, subs, side, scale)),
@@ -580,7 +593,7 @@
             jax.ShapeDtypeStruct(features.shape, jnp.bfloat16),
             jax.ShapeDtypeStruct((K, chans, filters.shape[2]), jnp.float32),
         ),
-        in_specs=[vmem, vmem, vmem, smem, smem, hbm, hbm, hbm],
+        in_specs=[hbm] * 8,
         out_specs=(vmem, vmem),
         scratch_shapes=[
             pltpu.VMEM((slots * tiles_n * 4, chans, width), jnp.bfloat16),
@@ -593,7 +606,11 @@
             pltpu.VMEM((slots,) + matrices.shape[1:], jnp.bfloat16),
             pltpu.VMEM(spread.shape, jnp.bfloat16),
             pltpu.VMEM(take.shape, jnp.bfloat16),
-            dma((2 + slots,)),
+            pltpu.VMEM(features.shape, jnp.bfloat16),
+            pltpu.VMEM(filters.shape, jnp.bfloat16),
+            pltpu.SMEM(tile_map.shape, jnp.int32),
+            pltpu.SMEM(table.shape, jnp.int32),
+            dma((7 + slots,)),
             dma((tiles_n,)),
             dma((tiles_n,)),
             dma((subs,)),
@@ -604,7 +621,7 @@
             dma((subs * tiles_n,)),
         ],
         compiler_params=pltpu.CompilerParams(
-            collective_id=0, has_side_effects=True, vmem_limit_bytes=40 * 2**20
+            collective_id=0, has_side_effects=True, vmem_limit_bytes=67043328
         ),
     )(
         features,

time: 28.3 us -> 22.5 us (0.80)
  local copies, waits for them, and re-layouts: 8.44 us -> 2.76 us
    unnamed x18 -> x2, local copies, waits for them, and re-layouts: 8.44 us -> 2.76 us
where the time goes in v2:
time: 22.5 us; the launch traced here: 22.3 us
  Pallas kernels  18.9 us (84%)
  local copies, waits for them, and re-layouts  2.76 us (12%)
  between operations  0.64 us (3%)
    pallas_call x1, Pallas kernels, face_path(): pl.pallas_call(functools.partial(face_kernel, (slots, tiles_n, subs, side...  18.9 us
    unnamed x2, local copies, waits for them, and re-layouts  2.76 us

profile of v2, /device:TPU:0, one launch (start us, length us, event | category | flops | bytes accessed | tf_op | source)
XLA Modules:
  0.0 22.3 jit_solution(5362723621431079393)
XLA Ops:
  0.6 18.9 %shard_map.95 = (bf16[3,8,1024]{2,1,0:T(8,128)(2,1)}, f32[5,8,32]{2,1,0:T(8,128)}) custom-call(bf16[3,8,1024]{2,1,0:T(8,128)(2,1)} %x_hbm.1, bf16[3,8,1024]{2,1,0:T(8,128)(2,1)} %g_hbm.1, bf16[5,32,32]{2,1,0:T(8,128)(2,1)} %f_hbm.1, s32[12]{0:T(128)} %map_hbm.1, s32[120]{0:T(128)} %constant.8.clone.table_hbm, s8[3,1280,512]{2,1,0:T(32,128)(4,1)} %constant.9.clone.ghost_hbm, ...), custom_call_target="tpu_custom_call" | custom-call | tf_op jit(solution)/shard_map/pallas_call | solution.py:590
  19.5 1.4 %copy.12 = bf16[3,8,1024]{2,1,0:T(8,128)(2,1)} copy(bf16[3,8,1024]{2,1,0:T(8,128)(2,1)} %get-tuple-element.4) | data formatting | bytes 98304
  20.9 1.3 %copy.13 = f32[5,8,32]{2,1,0:T(8,128)} copy(f32[5,8,32]{2,1,0:T(8,128)} %get-tuple-element.5) | data formatting | bytes 10240

commit v3 on v2

--- a/solution.py
+++ b/solution.py
@@ -324,6 +324,8 @@
     part_in,
     block,
     block_in,
+    summed,
+    summed_in,
     ghost_raw,
     ghost,
     spread,
@@ -341,6 +343,8 @@
     p_recv,
     w_send,
     w_recv,
+    t_send,
+    t_recv,
 ):
     slots, tiles_n, subs, side, scale = sizes
     chans = g_ref.shape[1]
@@ -348,13 +352,13 @@
     width = DEPTH * side
     j = lax.axis_index("tile")
     s = lax.axis_index("sub")
-    tile_peers = [lax.rem(j + d, tiles_n) for d in range(1, tiles_n)]
+    tile_peers = []
+    for d in range(tiles_n - 1):
+        up = d + (j <= d).astype(jnp.int32)
+        back = tiles_n - 2 - d
+        down = back + (j <= back).astype(jnp.int32)
+        tile_peers.append(jnp.where(2 * j < tiles_n, down, up))
     sub_peers = [lax.rem(s + d, subs) for d in range(1, subs)]
-    every = [(d, e) for d in range(tiles_n) for e in range(subs) if d + e > 0]
-
-    def device(d, e):
-        return {"tile": lax.rem(j + d, tiles_n), "sub": lax.rem(s + e, subs)}
-
     slot_loads = [
         pltpu.make_async_copy(map_hbm, map_ref, load_sem.at[0]),
         pltpu.make_async_copy(g_hbm, g_ref, load_sem.at[1]),
@@ -363,9 +367,10 @@
     for copy in slot_loads:
         copy.start()
     barrier = pltpu.get_barrier_semaphore()
-    for d, e in every:
+    friends = [{"tile": peer} for peer in tile_peers] + [{"sub": peer} for peer in sub_peers]
+    for friend in friends:
         pl.semaphore_signal(
-            barrier, inc=1, device_id=device(d, e), device_id_type=pl.DeviceIdType.MESH
+            barrier, inc=1, device_id=friend, device_id_type=pl.DeviceIdType.MESH
         )
     loads = [
         pltpu.make_async_copy(f_hbm, f_ref, load_sem.at[3]),
@@ -402,7 +407,7 @@
         strips[row + 1] = own[m][:, pixels - width :].astype(jnp.bfloat16)
         strips[row + 2] = cut[rows, :width].astype(jnp.bfloat16)
         strips[row + 3] = cut[rows, width:].astype(jnp.bfloat16)
-    pl.semaphore_wait(barrier, len(every))
+    pl.semaphore_wait(barrier, len(friends))
 
     def strip_copy(d, sender, target):
         mine = strips.at[pl.ds(sender * slots * 4, slots * 4)]
@@ -435,13 +440,23 @@
             device_id_type=pl.DeviceIdType.MESH,
         )
 
-    def block_copy(order, d, e, sender):
+    def block_copy(d, sender, target):
         return pltpu.make_async_remote_copy(
-            block.at[lax.rem(s + e, subs)],
+            block,
             block_in.at[sender],
-            w_send.at[order],
+            w_send.at[d],
             w_recv.at[sender],
-            device_id=device(d, e),
+            device_id={"tile": target},
+            device_id_type=pl.DeviceIdType.MESH,
+        )
+
+    def sum_copy(d, sender, target):
+        return pltpu.make_async_remote_copy(
+            summed.at[target],
+            summed_in.at[sender],
+            t_send.at[d],
+            t_recv.at[sender],
+            device_id={"sub": target},
             device_id_type=pl.DeviceIdType.MESH,
         )
 
@@ -539,10 +554,18 @@
     blocks = jnp.concatenate(sums, axis=1) * scale
     for e in range(subs):
         block[e] = blocks[e * chans : (e + 1) * chans]
-    me = j * subs + s
-    for order, (d, e) in enumerate(every):
-        block_copy(order, d, e, me).start()
-    block_in[me] = block[s]
+    for d, peer in enumerate(tile_peers):
+        block_copy(d, j, peer).start()
+    block_in[j] = block[...]
+    for d, peer in enumerate(tile_peers):
+        block_copy(d, peer, peer).wait_recv()
+    total = block_in[0]
+    for t in range(1, tiles_n):
+        total = total + block_in[t]
+    summed[...] = total
+    for d, peer in enumerate(sub_peers):
+        sum_copy(d, s, peer).start()
+    summed_in[s] = summed[s]
 
     for m in range(slots):
         for d, peer in enumerate(sub_peers):
@@ -555,26 +578,20 @@
             total = total + part_in[m, e]
         in_ref[slot] = total.astype(in_ref.dtype)
 
-    for order, (d, e) in enumerate(every):
-        sender = lax.rem(j + d, tiles_n) * subs + lax.rem(s + e, subs)
-        block_copy(order, d, e, sender).wait_recv()
-    whole = []
-    for e in range(subs):
-        total = block_in[e]
-        for t in range(1, tiles_n):
-            total = total + block_in[t * subs + e]
-        whole.append(total)
+    for d, peer in enumerate(sub_peers):
+        sum_copy(d, peer, peer).wait_recv()
     for k in range(K):
-        w_ref[k] = jnp.concatenate([v[:, k * chans : (k + 1) * chans] for v in whole], axis=1)
+        at = slice(k * chans, (k + 1) * chans)
+        w_ref[k] = jnp.concatenate([summed_in[e][:, at] for e in range(subs)], axis=1)
 
     for d, peer in enumerate(tile_peers):
         strip_copy(d, j, peer).wait_send()
+        block_copy(d, j, peer).wait_send()
     for d, peer in enumerate(sub_peers):
         x_copy(d, s, peer).wait_send()
         for m in range(slots):
             part_copy(m, d, s, peer).wait_send()
-    for order, (d, e) in enumerate(every):
-        block_copy(order, d, e, me).wait_send()
+        sum_copy(d, s, peer).wait_send()
 
 
 def face_path(features, out_grad, filters, tile_map):
@@ -601,7 +618,9 @@
             pltpu.VMEM((slots, subs, chans, pixels), jnp.float32),
             pltpu.VMEM((slots, subs, chans, pixels), jnp.float32),
             pltpu.VMEM((subs, chans, 128), jnp.float32),
-            pltpu.VMEM((subs * tiles_n, chans, 128), jnp.float32),
+            pltpu.VMEM((tiles_n, subs, chans, 128), jnp.float32),
+            pltpu.VMEM((subs, chans, 128), jnp.float32),
+            pltpu.VMEM((subs, chans, 128), jnp.float32),
             pltpu.VMEM((slots,) + matrices.shape[1:], jnp.int8),
             pltpu.VMEM((slots,) + matrices.shape[1:], jnp.bfloat16),
             pltpu.VMEM(spread.shape, jnp.bfloat16),
@@ -617,8 +636,10 @@
             dma((subs,)),
             dma((slots, subs)),
             dma((slots, subs)),
-            dma((subs * tiles_n,)),
-            dma((subs * tiles_n,)),
+            dma((tiles_n,)),
+            dma((tiles_n,)),
+            dma((subs,)),
+            dma((subs,)),
         ],
         compiler_params=pltpu.CompilerParams(
             collective_id=0, has_side_effects=True, vmem_limit_bytes=67043328

time: 22.5 us -> 23.8 us (1.058)
  Pallas kernels: 18.9 us -> 20.1 us
    pallas_call x1, Pallas kernels: 18.9 us -> 20.1 us  [face_path(): pl.pallas_call(functools.partial(face_kernel, (slots, tiles_n, subs, side...]
where the time goes in v3:
time: 23.8 us; the launch traced here: 23.5 us
  Pallas kernels  20.1 us (84%)
  local copies, waits for them, and re-layouts  2.76 us (12%)
  between operations  0.64 us (3%)
    pallas_call x1, Pallas kernels, face_path(): pl.pallas_call(functools.partial(face_kernel, (slots, tiles_n, subs, side...  20.1 us
    unnamed x2, local copies, waits for them, and re-layouts  2.76 us

profile of v3, /device:TPU:0, one launch (start us, length us, event | category | flops | bytes accessed | tf_op | source)
XLA Modules:
  0.0 23.5 jit_solution(10683309352735077554)
XLA Ops:
  0.6 20.1 %shard_map.95 = (bf16[3,8,1024]{2,1,0:T(8,128)(2,1)}, f32[5,8,32]{2,1,0:T(8,128)}) custom-call(bf16[3,8,1024]{2,1,0:T(8,128)(2,1)} %x_hbm.1, bf16[3,8,1024]{2,1,0:T(8,128)(2,1)} %g_hbm.1, bf16[5,32,32]{2,1,0:T(8,128)(2,1)} %f_hbm.1, s32[12]{0:T(128)} %map_hbm.1, s32[120]{0:T(128)} %constant.8.clone.table_hbm, s8[3,1280,512]{2,1,0:T(32,128)(4,1)} %constant.9.clone.ghost_hbm, ...), custom_call_target="tpu_custom_call" | custom-call | tf_op jit(solution)/shard_map/pallas_call | solution.py:607
  20.8 1.4 %copy.12 = bf16[3,8,1024]{2,1,0:T(8,128)(2,1)} copy(bf16[3,8,1024]{2,1,0:T(8,128)(2,1)} %get-tuple-element.4) | data formatting | bytes 98304
  22.2 1.3 %copy.13 = f32[5,8,32]{2,1,0:T(8,128)} copy(f32[5,8,32]{2,1,0:T(8,128)} %get-tuple-element.5) | data formatting | bytes 10240

commit v4 on v2

--- a/solution.py
+++ b/solution.py
@@ -348,7 +348,12 @@
     width = DEPTH * side
     j = lax.axis_index("tile")
     s = lax.axis_index("sub")
-    tile_peers = [lax.rem(j + d, tiles_n) for d in range(1, tiles_n)]
+    tile_peers = []
+    for d in range(tiles_n - 1):
+        up = d + (j <= d).astype(jnp.int32)
+        back = tiles_n - 2 - d
+        down = back + (j <= back).astype(jnp.int32)
+        tile_peers.append(jnp.where(2 * j < tiles_n, down, up))
     sub_peers = [lax.rem(s + d, subs) for d in range(1, subs)]
     every = [(d, e) for d in range(tiles_n) for e in range(subs) if d + e > 0]
 
@@ -451,6 +456,13 @@
         x_copy(d, s, peer).start()
 
     loads[0].wait()
+    def mix(m):
+        mixed = jnp.dot(mixing, terms[m], preferred_element_type=jnp.float32)
+        for e in range(subs):
+            part[m, e] = mixed[e * chans : (e + 1) * chans]
+        for d, peer in enumerate(sub_peers):
+            part_copy(m, d, s, peer).start()
+
     total_rows = (2 * K - 1) * chans
     row_k = lax.broadcasted_iota(jnp.int32, (subs * chans, total_rows), 1) // chans
     row_o = lax.broadcasted_iota(jnp.int32, (subs * chans, total_rows), 1) % chans
@@ -516,11 +528,8 @@
                 previous, current = current, -0.5 * around(current, k) - previous
         term = jnp.concatenate(held, axis=0).astype(jnp.bfloat16)
         terms.append(term)
-        mixed = jnp.dot(mixing, term, preferred_element_type=jnp.float32)
-        for e in range(subs):
-            part[m, e] = mixed[e * chans : (e + 1) * chans]
-        for d, peer in enumerate(sub_peers):
-            part_copy(m, d, s, peer).start()
+        if m < slots - 1:
+            mix(m)
 
     for d, peer in enumerate(sub_peers):
         x_copy(d, peer, peer).wait_recv()
@@ -542,6 +551,7 @@
     me = j * subs + s
     for order, (d, e) in enumerate(every):
         block_copy(order, d, e, me).start()
+    mix(slots - 1)
     block_in[me] = block[s]
 
     for m in range(slots):
@@ -590,8 +600,8 @@
     return pl.pallas_call(
         functools.partial(face_kernel, (slots, tiles_n, subs, side, scale)),
         out_shape=(
-            jax.ShapeDtypeStruct(features.shape, jnp.bfloat16),
-            jax.ShapeDtypeStruct((K, chans, filters.shape[2]), jnp.float32),
+            pltpu.VMEM(features.shape, jnp.bfloat16),
+            pltpu.VMEM((K, chans, filters.shape[2]), jnp.float32),
         ),
         in_specs=[hbm] * 8,
         out_specs=(vmem, vmem),
@@ -621,7 +631,7 @@
             dma((subs * tiles_n,)),
         ],
         compiler_params=pltpu.CompilerParams(
-            collective_id=0, has_side_effects=True, vmem_limit_bytes=67043328
+            collective_id=0, has_side_effects=True, vmem_limit_bytes=67043328 - 512 * 1024
         ),
     )(
         features,

time: 22.5 us -> 19.7 us (0.88)
  local copies, waits for them, and re-layouts: 2.76 us -> 1.23 us
  Pallas kernels: 18.9 us -> 17.6 us
    unnamed x2, local copies, waits for them, and re-layouts: 2.76 us -> 1.23 us
    pallas_call x1, Pallas kernels: 18.9 us -> 17.6 us  [face_path(): pl.pallas_call(functools.partial(face_kernel, (slots, tiles_n, subs, side...]
where the time goes in v4:
time: 19.7 us; the launch traced here: 19.5 us
  Pallas kernels  17.6 us (89%)
  local copies, waits for them, and re-layouts  1.23 us (6%)
  between operations  0.64 us (3%)
    pallas_call x1, Pallas kernels, face_path(): pl.pallas_call(functools.partial(face_kernel, (slots, tiles_n, subs, side...  17.6 us
    unnamed x2, local copies, waits for them, and re-layouts  1.23 us

profile of v4, /device:TPU:0, one launch (start us, length us, event | category | flops | bytes accessed | tf_op | source)
XLA Modules:
  0.0 19.5 jit_solution(4219146453044705934)
XLA Ops:
  0.6 17.6 %shard_map.95 = (bf16[3,8,1024]{2,1,0:T(8,128)(2,1)S(1)}, f32[5,8,32]{2,1,0:T(8,128)S(1)}) custom-call(bf16[3,8,1024]{2,1,0:T(8,128)(2,1)} %x_hbm.1, bf16[3,8,1024]{2,1,0:T(8,128)(2,1)} %g_hbm.1, bf16[5,32,32]{2,1,0:T(8,128)(2,1)} %f_hbm.1, s32[12]{0:T(128)} %map_hbm.1, s32[120]{0:T(128)} %constant.8.clone.table_hbm, ...), custom_call_target="tpu_custom_call" | custom-call | tf_op jit(solution)/shard_map/pallas_call | solution.py:600
  18.3 0.6 %copy.12 = bf16[3,8,1024]{2,1,0:T(8,128)(2,1)} copy(bf16[3,8,1024]{2,1,0:T(8,128)(2,1)S(1)} %get-tuple-element.2) | data formatting | bytes 98304
  18.9 0.6 %copy.13 = f32[5,8,32]{2,1,0:T(8,128)} copy(f32[5,8,32]{2,1,0:T(8,128)S(1)} %get-tuple-element.3) | data formatting | bytes 10240

commit v5 on v4

--- a/solution.py
+++ b/solution.py
@@ -332,6 +332,7 @@
     f_ref,
     map_ref,
     table_ref,
+    known,
     load_sem,
     s_send,
     s_recv,
@@ -368,9 +369,10 @@
     for copy in slot_loads:
         copy.start()
     barrier = pltpu.get_barrier_semaphore()
-    for d, e in every:
+    friends = [{"tile": peer} for peer in tile_peers] + [{"sub": peer} for peer in sub_peers]
+    for friend in friends:
         pl.semaphore_signal(
-            barrier, inc=1, device_id=device(d, e), device_id_type=pl.DeviceIdType.MESH
+            barrier, inc=1, device_id=friend, device_id_type=pl.DeviceIdType.MESH
         )
     loads = [
         pltpu.make_async_copy(f_hbm, f_ref, load_sem.at[3]),
@@ -407,7 +409,11 @@
         strips[row + 1] = own[m][:, pixels - width :].astype(jnp.bfloat16)
         strips[row + 2] = cut[rows, :width].astype(jnp.bfloat16)
         strips[row + 3] = cut[rows, width:].astype(jnp.bfloat16)
-    pl.semaphore_wait(barrier, len(every))
+    pl.semaphore_wait(barrier, len(friends))
+    for peer in sub_peers:
+        pl.semaphore_signal(
+            known, inc=1, device_id={"sub": peer}, device_id_type=pl.DeviceIdType.MESH
+        )
 
     def strip_copy(d, sender, target):
         mine = strips.at[pl.ds(sender * slots * 4, slots * 4)]
@@ -549,6 +555,7 @@
     for e in range(subs):
         block[e] = blocks[e * chans : (e + 1) * chans]
     me = j * subs + s
+    pl.semaphore_wait(known, subs - 1)
     for order, (d, e) in enumerate(every):
         block_copy(order, d, e, me).start()
     mix(slots - 1)
@@ -620,6 +627,7 @@
             pltpu.VMEM(filters.shape, jnp.bfloat16),
             pltpu.SMEM(tile_map.shape, jnp.int32),
             pltpu.SMEM(table.shape, jnp.int32),
+            pltpu.SemaphoreType.REGULAR,
             dma((7 + slots,)),
             dma((tiles_n,)),
             dma((tiles_n,)),

time: 19.7 us -> 19.4 us (0.985)
  Pallas kernels: 17.6 us -> 17.4 us
    pallas_call x1, Pallas kernels: 17.6 us -> 17.4 us  [face_path(): pl.pallas_call(functools.partial(face_kernel, (slots, tiles_n, subs, side...]
where the time goes in v5:
time: 19.4 us; the launch traced here: 19.3 us
  Pallas kernels  17.4 us (90%)
  local copies, waits for them, and re-layouts  1.23 us (6%)
  between operations  0.64 us (3%)
    pallas_call x1, Pallas kernels, face_path(): pl.pallas_call(functools.partial(face_kernel, (slots, tiles_n, subs, side...  17.4 us
    unnamed x2, local copies, waits for them, and re-layouts  1.23 us

profile of v5, /device:TPU:0, one launch (start us, length us, event | category | flops | bytes accessed | tf_op | source)
XLA Modules:
  0.0 19.3 jit_solution(16614602395228427958)
XLA Ops:
  0.6 17.4 %shard_map.95 = (bf16[3,8,1024]{2,1,0:T(8,128)(2,1)S(1)}, f32[5,8,32]{2,1,0:T(8,128)S(1)}) custom-call(bf16[3,8,1024]{2,1,0:T(8,128)(2,1)} %x_hbm.1, bf16[3,8,1024]{2,1,0:T(8,128)(2,1)} %g_hbm.1, bf16[5,32,32]{2,1,0:T(8,128)(2,1)} %f_hbm.1, s32[12]{0:T(128)} %map_hbm.1, s32[120]{0:T(128)} %constant.8.clone.table_hbm, ...), custom_call_target="tpu_custom_call" | custom-call | tf_op jit(solution)/shard_map/pallas_call | solution.py:607
  18.1 0.6 %copy.12 = bf16[3,8,1024]{2,1,0:T(8,128)(2,1)} copy(bf16[3,8,1024]{2,1,0:T(8,128)(2,1)S(1)} %get-tuple-element.2) | data formatting | bytes 98304
  18.7 0.6 %copy.13 = f32[5,8,32]{2,1,0:T(8,128)} copy(f32[5,8,32]{2,1,0:T(8,128)S(1)} %get-tuple-element.3) | data formatting | bytes 10240
